TPU v7x, 256 devices: a whole 4x4x8 slice. The times are simulated.
256 devices in a mesh: seq: 8 (over z), head: 4 (over y_hi, core), rep: 8 (over y_lo, x).
Axes of the slice: x: 4, y: 4 (y_hi: 2, y_lo: 2; y = y_hi * 2 + y_lo), z: 8, core: 2. Of those that a mesh axis runs over, the one named last changes fastest.
Arguments:
- queries: bfloat16 [8, 2048, 7168], P('rep', 'seq', 'head'), may hold values from -6 to 6
- new_keys: bfloat16 [8, 2048, 7168], P('rep', 'seq', 'head'), may hold values from -6 to 6
- new_values: bfloat16 [8, 2048, 7168], P('rep', 'seq', 'head'), may hold values from -4 to 4
- lengths: int32 [8, 4], P('rep'), may hold values from 1 to 1024, 2048 in all within a row
- offsets: int32 [8, 4], P('rep'), may hold values from 0 to 4095
- slot_map: int32 [8, 4], P('rep'), may hold values from 0 to 3, each once within a row
Outputs:
- attended: bfloat16 [8, 2048, 7168], P('rep', 'seq', 'head')
- key_cache: bfloat16 [8, 4, 1024, 7168], P('rep', 'head', None, 'seq')
- value_cache: bfloat16 [8, 4, 1024, 7168], P('rep', 'head', None, 'seq')
Inputs may be any that keep to these rules, and one draw needn't show every extreme that they name: `lengths`: each row sums to 2048; its first entry is the group's shared prompt; every row has one entry equal to 1024. `slot_map`: each row is a permutation of the group's requests.
All inputs are finite; a program needn't handle non-finite values.
Results may differ from a plain program's by a relative error of at most 0.011.
Values may be sent and summed in bfloat16 or wider, within the bound.
A program may use at most 128 MiB of HBM per device.

v0:
```python
import math
import jax
import jax.numpy as jnp
from jax import lax
from jax.sharding import PartitionSpec as P

HD = 224
NEG_FILL = -1e30
ROPE_BASE = 10000.0
KEY_BLOCK = 512


def rotate(source, places):
    full_width = source.shape[-1]
    half_width = full_width // 2
    inverse = jnp.power(
        jnp.float32(ROPE_BASE), -2.0 * jnp.arange(half_width, dtype=jnp.float32) / full_width
    )
    angles = places.astype(jnp.float32)[:, None] * inverse[None, :]
    cosine = jnp.cos(angles)[:, None, :]
    sine_terms = jnp.sin(angles)[:, None, :]
    first_part = source[..., :half_width].astype(jnp.float32)
    second_part = source[..., half_width:].astype(jnp.float32)
    rotated = jnp.concatenate(
        [
            first_part * cosine - second_part * sine_terms,
            second_part * cosine + first_part * sine_terms,
        ],
        axis=-1,
    )
    return rotated.astype(jnp.bfloat16)


def token_request(token_ids, ends_at):
    return jnp.sum((token_ids[:, None] >= ends_at[None, :]).astype(jnp.int32), axis=1)


def lookup_rows(request, lookup):
    matches = request[:, None] == jnp.arange(lookup.shape[0], dtype=jnp.int32)[None, :]
    return jnp.sum(jnp.where(matches, lookup[None, :], 0), axis=1)


def empty_state(head_count, row_count):
    return (
        jnp.full((head_count, row_count), NEG_FILL, jnp.float32),
        jnp.zeros((head_count, row_count), jnp.float32),
        jnp.zeros((head_count, row_count, HD), jnp.float32),
    )


def finish(running):
    row_best, row_total, summed = running
    head_count, row_count, _ = summed.shape
    return (
        (summed / row_total[:, :, None])
        .transpose(1, 0, 2)
        .reshape(row_count, head_count * HD)
        .astype(jnp.bfloat16)
    )


def update(
    running, query_token_rows, query_tok, query_req, key_rows, value_rows, key_start, ends_at
):
    row_count = key_rows.shape[0]
    head_count = query_token_rows.shape[1]
    key_token_index = key_start + jnp.arange(row_count, dtype=jnp.int32)
    key_req = token_request(key_token_index, ends_at)
    same_request = (key_req[None, :] == query_req[:, None]) & (
        key_token_index[None, :] <= query_tok[:, None]
    )
    prompt_keys = (key_req[None, :] == 0) & (query_req[:, None] != 0)
    allowed = same_request | prompt_keys
    row_best, row_total, summed = running
    key_head_stack = key_rows.reshape(row_count, head_count, HD)
    value_heads = value_rows.reshape(row_count, head_count, HD)
    scores = jnp.einsum(
        "ezq,izq->zei", query_token_rows, key_head_stack, preferred_element_type=jnp.float32
    ) * (1.0 / math.sqrt(HD))
    scores = jnp.where(allowed[None], scores, NEG_FILL)
    best_new = jnp.maximum(row_best, jnp.max(scores, axis=2))
    factor = jnp.exp(row_best - best_new)
    weights = jnp.where(allowed[None], jnp.exp(scores - best_new[:, :, None]), 0.0)
    total_new = row_total * factor + jnp.sum(weights, axis=2)
    mixed = jnp.einsum(
        "eva,ael->evl",
        weights.astype(jnp.bfloat16),
        value_heads,
        preferred_element_type=jnp.float32,
    )
    return (best_new, total_new, summed * factor[:, :, None] + mixed)


def per_device(queries, new_keys, new_values, lengths, offsets, slot_map):
    tok_dev = queries.shape[1]
    local_cols = queries.shape[2]
    head_count = local_cols // HD
    tokens_total = tok_dev * lax.axis_size("seq")
    cache_len = tokens_total // 2
    lengths_row = lengths[0]
    offsets_row = offsets[0]
    slots_row = slot_map[0]
    request_count = lengths_row.shape[0]
    ends_at = jnp.cumsum(lengths_row)
    begins = ends_at - lengths_row
    token_ids = lax.axis_index("seq") * tok_dev + jnp.arange(tok_dev, dtype=jnp.int32)
    request = token_request(token_ids, ends_at)
    places = lookup_rows(request, offsets_row) + token_ids - lookup_rows(request, begins)
    rot_queries = rotate(queries[0].reshape(tok_dev, head_count, HD), places)
    rot_keys = rotate(new_keys[0].reshape(tok_dev, head_count, HD), places).reshape(
        tok_dev, local_cols
    )
    value_rows = new_values[0]
    key_rows = lax.all_gather(rot_keys, "seq", axis=0, tiled=True)
    piece_values = lax.all_gather(value_rows, "seq", axis=0, tiled=True)
    row_count = key_rows.shape[0]

    def key_step(key_index, state_in):
        first_row = key_index * KEY_BLOCK
        return update(
            state_in,
            rot_queries,
            token_ids,
            request,
            lax.dynamic_slice_in_dim(key_rows, first_row, KEY_BLOCK, 0),
            lax.dynamic_slice_in_dim(piece_values, first_row, KEY_BLOCK, 0),
            first_row,
            ends_at,
        )

    finished = lax.fori_loop(0, row_count // KEY_BLOCK, key_step, empty_state(head_count, tok_dev))
    attended = finish(finished)
    stacked = jnp.stack([rot_keys, value_rows])
    my_slot = lax.axis_index("head")
    request_ids = jnp.arange(request_count, dtype=jnp.int32)
    owner = jnp.sum(jnp.where(slots_row == my_slot, request_ids, 0))
    owner_begin = jnp.sum(jnp.where(request_ids == owner, begins, 0))
    slot_of = lookup_rows(request, slots_row)
    member = slot_of[None, :] == request_ids[:, None]
    buckets = jnp.where(member[None, :, :, None], stacked[:, None], jnp.zeros((), jnp.bfloat16))
    moved = lax.all_to_all(
        lax.all_to_all(buckets, "head", split_axis=1, concat_axis=3, tiled=True),
        "seq",
        split_axis=3,
        concat_axis=2,
        tiled=True,
    )
    padded = jnp.concatenate(
        [moved, jnp.zeros((2, 1, cache_len, moved.shape[3]), jnp.bfloat16)], axis=2
    )
    window = lax.dynamic_slice_in_dim(padded, owner_begin, cache_len, 2)
    return (attended[None], window[0:1], window[1:2])


def solution(mesh):
    in_specs = (
        P("rep", "seq", "head"),
        P("rep", "seq", "head"),
        P("rep", "seq", "head"),
        P("rep", None),
        P("rep", None),
        P("rep", None),
    )
    out_specs = (
        P("rep", "seq", "head"),
        P("rep", "head", None, "seq"),
        P("rep", "head", None, "seq"),
    )
    return jax.shard_map(
        per_device, mesh=mesh, in_specs=in_specs, out_specs=out_specs, check_vma=False
    )
```

profile of v0, /device:TPU:96, one launch (start us, length us, event | category | flops | bytes accessed | tf_op | source)
XLA Modules:
  0.0 385.8 jit_solution(3452643616625133445)
XLA Ops:
  7.2 0.0 all-gather.4.cloned.1.call-start
  7.3 0.9 reduce-window.4
  8.1 0.7 fusion.29
  8.8 1.5 copy.46
  10.3 0.1 convert_reduce_fusion.1
  10.4 0.8 select_reduce_fusion
  11.1 0.5 multiply_cosine_fusion
  11.6 0.3 fusion.21
  11.9 1.0 maximum_convert_fusion
  12.9 0.0 all-gather.4.cloned.1.call-update
  12.9 0.0 all-gather.6.cloned.1.call-start
  13.0 1.3 copy.48
  14.3 0.0 all-gather.6.cloned.1.call-update
  14.3 0.6 copy.49
  14.9 1.4 pad_maximum_fusion
  16.3 2.8 copy.50
  19.1 3.4 broadcast_select_fusion
  22.6 5.6 %all-to-all-start = ((bf16[2,4,256,1792]{2,3,0,1:T(8,128)(2,1)}), bf16[2,4,256,1792]{2,3,0,1:T(8,128)(2,1)}, u32[]{:S(2)}, u32[]{:S(2)}) async-start(bf16[2,4,256,1792]{2,3,0,1:T(8,128)(2,1)} %broadcast_select_fusion), calls=%async_computation | async-start | bytes 14680064 | tf_op jit(solution)/shard_map/all_to_all | solution.py:142
  28.2 0.5 copy.47
  28.8 0.7 fusion.27
  29.5 0.0 copy-done.4
  29.5 1.3 fusion.28
  32.6 0.3 fusion.24
  32.9 0.1 pad_maximum_fusion.1
  33.0 78.6 %all-to-all-done = bf16[2,4,256,1792]{2,3,0,1:T(8,128)(2,1)} async-done(((bf16[2,4,256,1792]{2,3,0,1:T(8,128)(2,1)}), bf16[2,4,256,1792]{2,3,0,1:T(8,128)(2,1)}, u32[]{:S(2)}, u32[]{:S(2)}) %all-to-all-start) | async-done | bytes 7340064 | tf_op jit(solution)/shard_map/all_to_all | solution.py:142
  111.6 3.6 copy.51
  115.2 47.2 %copy.52 = bf16[2,1,256,7168]{2,0,1,3:T(2,128)(2,1)} copy(bf16[2,1,256,7168]{2,3,0,1:T(8,128)(2,1)S(1)} %bitcast.73) | data formatting | bytes 14680064 | tf_op jit(solution)/shard_map/all_to_all | solution.py:142
  162.3 7.7 %all-to-all-start.1 = ((bf16[2,1,256,7168]{2,0,1,3:T(2,128)(2,1)}), bf16[2,1,256,7168]{2,0,1,3:T(2,128)(2,1)}, u32[]{:S(2)}, u32[]{:S(2)}) async-start(bf16[2,1,256,7168]{2,0,1,3:T(2,128)(2,1)} %copy.52), calls=%async_computation.1 | async-start | bytes 14680064 | tf_op jit(solution)/shard_map/all_to_all | solution.py:141
  170.0 106.1 %all-gather.6.cloned.1.call-done = bf16[1,2048,1792]{1,2,0:T(8,128)(2,1)} async-done(((bf16[1,256,1792]{1,2,0:T(8,128)(2,1)}), bf16[1,2048,1792]{1,2,0:T(8,128)(2,1)}) %all-gather.6.cloned.1.call-update) | async-done | bytes 7340048 | tf_op jit(solution)/shard_map/all_gather | solution.py:115
  276.2 51.9 %while.18 = (s32[]{:T(128)}, f32[8,256]{1,0:T(8,128)S(1)}, f32[8,256]{1,0:T(8,128)S(1)}, f32[8,256,224]{1,2,0:T(8,128)}, s32[4]{0:T(128)S(1)}, /*index=5*/s32[25...) while((s32[]{:T(128)}, f32[8,256]{1,0:T(8,128)S(1)}, ...), condition=%wide.region_8.9_spmd.clone, body=%wide.region_4.8_spmd.clone.sunk | while | flops 955204608 | bytes 45631228 | solution.py:131
  276.2 0.1 convert_reduce_fusion.3
  276.3 0.3 and_or_fusion.2
  276.6 2.3 constant_dynamic-slice_fusion.3
  278.9 3.1 fusion.45
  281.9 3.3 fusion.46
  285.3 0.1 copy-done
  285.4 2.6 fusion.48
  288.0 0.1 convert_reduce_fusion.3
  288.1 0.3 and_or_fusion.2
  288.4 2.3 constant_dynamic-slice_fusion.3
  290.7 3.1 fusion.45
  293.8 3.3 fusion.46
  297.2 0.1 copy-done
  297.2 4.1 %fusion.48 = f32[8,256,224]{1,2,0:T(8,128)} fusion(f32[8,256,224]{1,2,0:T(8,128)} %get-tuple-element.350, bf16[512,8,224]{0,2,1:T(8,128)(2,1)S(1)} %bitcast.71, f32[8,512,256]{2,1,0:T(8,128)S(1)} %copy-done, f32[8,256]{1,0:T(8,128)S(1)} %select_maximum_fusion.2, pred[256,512]{0,1:T(8,128)(4,1)S(1)} %and_or_fusion.2, ...), kind=kOutput, calls=%fused_computation.13.clone.1 | convolution fusion | flops 476381184 | bytes 9846785 | tf_op jit(solution)/shard_map/while/body/eval_jaxpr/eva,ael->evl/dot_general | solution.py:85
  301.4 0.1 convert_reduce_fusion.3
  301.5 0.3 and_or_fusion.2
  301.8 2.3 constant_dynamic-slice_fusion.3
  304.1 3.1 fusion.45
  307.2 3.3 fusion.46
  310.5 0.1 copy-done
  310.6 4.1 %fusion.48 = f32[8,256,224]{1,2,0:T(8,128)} fusion(f32[8,256,224]{1,2,0:T(8,128)} %get-tuple-element.350, bf16[512,8,224]{0,2,1:T(8,128)(2,1)S(1)} %bitcast.71, f32[8,512,256]{2,1,0:T(8,128)S(1)} %copy-done, f32[8,256]{1,0:T(8,128)S(1)} %select_maximum_fusion.2, pred[256,512]{0,1:T(8,128)(4,1)S(1)} %and_or_fusion.2, ...), kind=kOutput, calls=%fused_computation.13.clone.1 | convolution fusion | flops 476381184 | bytes 9846785 | tf_op jit(solution)/shard_map/while/body/eval_jaxpr/eva,ael->evl/dot_general | solution.py:85
  314.7 0.1 convert_reduce_fusion.3
  314.8 0.3 and_or_fusion.2
  315.1 2.3 constant_dynamic-slice_fusion.3
  317.4 3.1 fusion.45
  320.5 3.3 fusion.46
  323.9 0.1 copy-done
  323.9 4.1 %fusion.48 = f32[8,256,224]{1,2,0:T(8,128)} fusion(f32[8,256,224]{1,2,0:T(8,128)} %get-tuple-element.350, bf16[512,8,224]{0,2,1:T(8,128)(2,1)S(1)} %bitcast.71, f32[8,512,256]{2,1,0:T(8,128)S(1)} %copy-done, f32[8,256]{1,0:T(8,128)S(1)} %select_maximum_fusion.2, pred[256,512]{0,1:T(8,128)(4,1)S(1)} %and_or_fusion.2, ...), kind=kOutput, calls=%fused_computation.13.clone.1 | convolution fusion | flops 476381184 | bytes 9846785 | tf_op jit(solution)/shard_map/while/body/eval_jaxpr/eva,ael->evl/dot_general | solution.py:85
  328.1 1.6 divide_convert_fusion
  329.7 1.4 copy.55
  331.1 24.2 %all-to-all-done.1 = bf16[2,1,256,7168]{2,0,1,3:T(2,128)(2,1)} async-done(((bf16[2,1,256,7168]{2,0,1,3:T(2,128)(2,1)}), bf16[2,1,256,7168]{2,0,1,3:T(2,128)(2,1)}, u32[]{:S(2)}, u32[]{:S(2)}) %all-to-all-start.1) | async-done | bytes 7340064 | tf_op jit(solution)/shard_map/all_to_all | solution.py:141
  355.3 7.0 %copy.53 = bf16[2,1,256,7168]{2,3,0,1:T(8,128)(2,1)} copy(bf16[2,1,256,7168]{2,0,1,3:T(2,128)(2,1)} %all-to-all-done.1) | data formatting | bytes 14680064 | tf_op jit(solution)/shard_map/all_to_all | solution.py:141
  362.3 11.1 %copy.54 = bf16[2,1,8,256,896]{4,3,2,0,1:T(8,128)(2,1)} copy(bf16[2,1,8,256,896]{3,4,2,0,1:T(8,128)(2,1)} %bitcast.74) | data formatting | bytes 14680064 | tf_op jit(solution)/shard_map/all_to_all | solution.py:141
  373.4 5.6 %fusion.19 = (bf16[1,1,1024,896]{3,2,1,0:T(8,128)(2,1)}, bf16[1,1,1024,896]{3,2,1,0:T(8,128)(2,1)}) fusion(s32[]{:T(128)S(6)} %add.111, s32[]{:T(128)S(6)} %select_n.53, bf16[2,1,2048,896]{3,2,0,1:T(8,128)(2,1)} %bitcast.75), kind=kLoop, calls=%fused_computation.32 | loop fusion | bytes 11010056
  (49 shorter events, 0.2 us)
Async XLA Ops:
  7.2 5.8 %copy-start.2 = (bf16[1,256,1792]{2,1,0:T(8,128)(2,1)S(1)}, bf16[1,256,1792]{2,1,0:T(8,128)(2,1)}, u32[]{:S(2)}) copy-start(bf16[1,256,1792]{2,1,0:T(8,128)(2,1)} %param.10) | copy-start | bytes 2752516
  7.2 162.8 %all-gather.4.cloned.1.call-start = ((), (), s32[]{:S(2)}) async-start(), calls=%async_computation.2 | async-start | bytes 8257536 | tf_op jit(solution)/shard_map/all_gather | solution.py:114
  12.9 1.4 copy-start.1
  12.9 263.2 %all-gather.6.cloned.1.call-start = ((), (), s32[]{:S(2)}) async-start(), calls=%async_computation.3 | async-start | bytes 8257536 | tf_op jit(solution)/shard_map/all_gather | solution.py:115
  22.6 5.6 %copy-start.3 = (bf16[1,256,1792]{2,1,0:T(8,128)(2,1)S(1)}, bf16[1,256,1792]{2,1,0:T(8,128)(2,1)}, u32[]{:S(2)}) copy-start(bf16[1,256,1792]{2,1,0:T(8,128)(2,1)} %param.8) | copy-start | bytes 2752516
  22.6 6.2 %copy-start.5 = (s32[1,4]{1,0:T(1,128)S(1)}, s32[1,4]{1,0:T(1,128)}, u32[]{:S(2)}) copy-start(s32[1,4]{1,0:T(1,128)} %param.13) | copy-start | bytes 52
  22.6 6.9 %copy-start.4 = (s32[1,4]{1,0:T(1,128)S(1)}, s32[1,4]{1,0:T(1,128)}, u32[]{:S(2)}) copy-start(s32[1,4]{1,0:T(1,128)} %param.11) | copy-start | bytes 52
  22.6 89.0 %all-to-all-start = ((bf16[2,4,256,1792]{2,3,0,1:T(8,128)(2,1)}), bf16[2,4,256,1792]{2,3,0,1:T(8,128)(2,1)}, u32[]{:S(2)}, u32[]{:S(2)}) async-start(bf16[2,4,256,1792]{2,3,0,1:T(8,128)(2,1)} %broadcast_select_fusion), calls=%async_computation | async-start | bytes 14680064 | tf_op jit(solution)/shard_map/all_to_all | solution.py:142
  162.3 192.9 %all-to-all-start.1 = ((bf16[2,1,256,7168]{2,0,1,3:T(2,128)(2,1)}), bf16[2,1,256,7168]{2,0,1,3:T(2,128)(2,1)}, u32[]{:S(2)}, u32[]{:S(2)}) async-start(bf16[2,1,256,7168]{2,0,1,3:T(2,128)(2,1)} %copy.52), calls=%async_computation.1 | async-start | bytes 14680064 | tf_op jit(solution)/shard_map/all_to_all | solution.py:141
  281.9 3.4 copy-start
  293.8 3.4 copy-start
  307.1 3.4 copy-start
  320.5 3.4 copy-start
Sparse Core Ops, SparseCore 0:
  13.1 91.4 all-gather.3
  106.8 169.2 all-gather.5
where the time goes:
time: 387 us; the launch traced here: 386 us
  waiting for transfers between devices  209 us (54%)
  local copies, waits for them, and re-layouts  92 us (24%)
  other arithmetic  28 us (7%)
  matrix products  27.3 us (7%)
  between operations  16.1 us (4%)
  starting transfers between devices  13.3 us (3%)
    all_gather x1, waiting for transfers between devices, per_device(): piece_values = lax.all_gather(value_rows, 'seq', axis=0, tiled=True)  106 us
    all_to_all x1, waiting for transfers between devices, per_device(): lax.all_to_all(buckets, 'head', split_axis=1, concat_axis=3, tiled=True)  78.6 us
    all_to_all x2, local copies, waits for them, and re-layouts, per_device(): lax.all_to_all(buckets, 'head', split_axis=1, concat_axis=3, tiled=True)  50.7 us
    all_to_all x1, waiting for transfers between devices, per_device(): lax.all_to_all(lax.all_to_all(buckets, 'head', split_axis=1, concat_axis=...  24.2 us
    all_to_all x2, local copies, waits for them, and re-layouts, per_device(): lax.all_to_all(lax.all_to_all(buckets, 'head', split_axis=1, concat_axis=...  18.1 us
    dot_general x4, matrix products, update(): jnp.einsum('eva,ael->evl', weights.astype(jnp.bfloat16), value_heads, pre...  15 us
    reduce_sum x4, other arithmetic, update(): total_new = row_total * factor + jnp.sum(weights, axis=2)  13.3 us
    dot_general x4, matrix products, update(): jnp.einsum('ezq,izq->zei', query_token_rows, key_head_stack, preferred_el...  12.3 us
  transfers between devices with their start and end apart: 4, of which 3 were waited for; matrix products, arithmetic and copies ran while one was open for 31% of the time, Pallas kernels for 0%

commit v1 on v0

--- a/solution.py
+++ b/solution.py
@@ -112,7 +112,9 @@
     )
     value_rows = new_values[0]
     key_rows = lax.all_gather(rot_keys, "seq", axis=0, tiled=True)
-    piece_values = lax.all_gather(value_rows, "seq", axis=0, tiled=True)
+    piece_values = jnp.concatenate(
+        lax.all_to_all(jnp.stack([value_rows] * lax.axis_size("seq")), "seq", 0, 0), axis=0
+    )
     row_count = key_rows.shape[0]
 
     def key_step(key_index, state_in):

time: 387 us -> 546 us (1.41); the launches traced: 386 us -> 539 us
  waiting for transfers between devices: 209 us -> 309 us
  local copies, waits for them, and re-layouts: 92 us -> 118 us
  starting transfers between devices: 13.3 us -> 34.5 us
  matrix products: 27.3 us -> 35.3 us
    all_to_all x0 -> x1, waiting for transfers between devices: none -> 151 us  [per_device(): lax.all_to_all(jnp.stack([value_rows] * lax.axis_size('seq')), 'seq', 0, 0)]
    all_gather x1 -> x0, waiting for transfers between devices: 106 us -> none  [per_device(): piece_values = lax.all_gather(value_rows, 'seq', axis=0, tiled=True)]
    all_to_all x1, waiting for transfers between devices: 24.2 us -> 73.8 us  [per_device(): lax.all_to_all(lax.all_to_all(buckets, 'head', split_axis=1, concat_axis=...]
    all_to_all x1, starting transfers between devices: 7.67 us -> 21.1 us  [per_device(): lax.all_to_all(lax.all_to_all(buckets, 'head', split_axis=1, concat_axis=...]
    all_to_all x0 -> x1, local copies, waits for them, and re-layouts: none -> 10.1 us  [per_device(): lax.all_to_all(jnp.stack([value_rows] * lax.axis_size('seq')), 'seq', 0, 0)]
    all_to_all x0 -> x1, starting transfers between devices: none -> 7.79 us  [per_device(): lax.all_to_all(jnp.stack([value_rows] * lax.axis_size('seq')), 'seq', 0, 0)]
    dot_general x4, matrix products: 15 us -> 22.7 us  [update(): jnp.einsum('eva,ael->evl', weights.astype(jnp.bfloat16), value_heads, pre...]
    dynamic_slice x4 -> x8, local copies, waits for them, and re-layouts: 9.24 us -> 15.8 us  [key_step(): lax.dynamic_slice_in_dim(piece_values, first_row, KEY_BLOCK, 0)]
  transfers between devices with their start and end apart: 4 -> 4, of which waited for: 3 -> 3; matrix products, arithmetic and copies ran while one was open for 31% -> 26% of each run, Pallas kernels for 0% -> 0%
where the time goes in v1:
time: 546 us; the launch traced here: 539 us
  waiting for transfers between devices  309 us (57%)
  local copies, waits for them, and re-layouts  118 us (22%)
  matrix products  35.3 us (6%)
  starting transfers between devices  34.5 us (6%)
  other arithmetic  26.4 us (5%)
  between operations  16.1 us (3%)
    all_to_all x1, waiting for transfers between devices, per_device(): lax.all_to_all(jnp.stack([value_rows] * lax.axis_size('seq')), 'seq', 0, 0)  151 us
    all_to_all x1, waiting for transfers between devices, per_device(): lax.all_to_all(buckets, 'head', split_axis=1, concat_axis=3, tiled=True)  82.9 us
    all_to_all x1, waiting for transfers between devices, per_device(): lax.all_to_all(lax.all_to_all(buckets, 'head', split_axis=1, concat_axis=...  73.8 us
    all_to_all x2, local copies, waits for them, and re-layouts, per_device(): lax.all_to_all(buckets, 'head', split_axis=1, concat_axis=3, tiled=True)  50.7 us
    dot_general x4, matrix products, update(): jnp.einsum('eva,ael->evl', weights.astype(jnp.bfloat16), value_heads, pre...  22.7 us
    all_to_all x1, starting transfers between devices, per_device(): lax.all_to_all(lax.all_to_all(buckets, 'head', split_axis=1, concat_axis=...  21.1 us
    all_to_all x2, local copies, waits for them, and re-layouts, per_device(): lax.all_to_all(lax.all_to_all(buckets, 'head', split_axis=1, concat_axis=...  18.1 us
    dynamic_slice x8, local copies, waits for them, and re-layouts, key_step(): lax.dynamic_slice_in_dim(piece_values, first_row, KEY_BLOCK, 0)  15.8 us
  transfers between devices with their start and end apart: 4, of which 3 were waited for; matrix products, arithmetic and copies ran while one was open for 26% of the time, Pallas kernels for 0%

profile of v1, /device:TPU:96, one launch (start us, length us, event | category | flops | bytes accessed | tf_op | source)
XLA Modules:
  0.0 539.0 jit_solution(14633590088818679633)
XLA Ops:
  7.2 0.9 reduce-window.4
  8.1 0.7 fusion.29
  8.8 1.5 copy.61
  10.3 0.8 select_reduce_fusion
  11.1 0.5 multiply_cosine_fusion
  11.6 0.3 fusion.21
  12.0 0.6 copy.66
  12.6 1.4 pad_maximum_fusion
  14.0 2.8 copy.67
  16.8 3.5 broadcast_select_fusion
  20.3 5.7 %all-to-all-start.1 = ((bf16[2,4,256,1792]{2,3,0,1:T(8,128)(2,1)}), bf16[2,4,256,1792]{2,3,0,1:T(8,128)(2,1)}, u32[]{:S(2)}, u32[]{:S(2)}) async-start(bf16[2,4,256,1792]{2,3,0,1:T(8,128)(2,1)} %broadcast_select_fusion), calls=%async_computation.1 | async-start | bytes 14680064 | tf_op jit(solution)/shard_map/all_to_all | solution.py:144
  25.9 0.5 copy.63
  26.5 82.9 %all-to-all-done.1 = bf16[2,4,256,1792]{2,3,0,1:T(8,128)(2,1)} async-done(((bf16[2,4,256,1792]{2,3,0,1:T(8,128)(2,1)}), bf16[2,4,256,1792]{2,3,0,1:T(8,128)(2,1)}, u32[]{:S(2)}, u32[]{:S(2)}) %all-to-all-start.1) | async-done | bytes 7340064 | tf_op jit(solution)/shard_map/all_to_all | solution.py:144
  109.4 3.4 stack.6
  112.8 7.8 %all-to-all-start = ((bf16[8,256,1792]{1,2,0:T(8,128)(2,1)}), bf16[8,256,1792]{1,2,0:T(8,128)(2,1)}, u32[]{:S(2)}, u32[]{:S(2)}) async-start(bf16[8,256,1792]{1,2,0:T(8,128)(2,1)} %stack.6), calls=%async_computation | async-start | bytes 14680064 | tf_op jit(solution)/shard_map/all_to_all | solution.py:116
  120.6 0.7 all-gather.2.cloned.1.call-update
  121.4 0.5 copy.62
  121.9 0.6 fusion.27
  122.6 1.3 fusion.28
  125.8 0.3 fusion.24
  126.2 3.6 copy.68
  129.7 47.2 %copy.69 = bf16[2,1,256,7168]{2,0,1,3:T(2,128)(2,1)} copy(bf16[2,1,256,7168]{2,3,0,1:T(8,128)(2,1)S(1)} %bitcast.75) | data formatting | bytes 14680064 | tf_op jit(solution)/shard_map/all_to_all | solution.py:144
  176.9 151.4 %all-to-all-done = bf16[8,256,1792]{1,2,0:T(8,128)(2,1)} async-done(((bf16[8,256,1792]{1,2,0:T(8,128)(2,1)}), bf16[8,256,1792]{1,2,0:T(8,128)(2,1)}, u32[]{:S(2)}, u32[]{:S(2)}) %all-to-all-start) | async-done | bytes 7340064 | tf_op jit(solution)/shard_map/all_to_all | solution.py:116
  328.4 21.1 %all-to-all-start.2 = ((bf16[2,1,256,7168]{2,0,1,3:T(2,128)(2,1)}), bf16[2,1,256,7168]{2,0,1,3:T(2,128)(2,1)}, u32[]{:S(2)}, u32[]{:S(2)}) async-start(bf16[2,1,256,7168]{2,0,1,3:T(2,128)(2,1)} %copy.69), calls=%async_computation.2 | async-start | bytes 14680064 | tf_op jit(solution)/shard_map/all_to_all | solution.py:143
  349.5 10.1 %copy.64 = bf16[8,256,1792]{2,1,0:T(8,128)(2,1)} copy(bf16[8,256,1792]{1,2,0:T(8,128)(2,1)} %all-to-all-done) | data formatting | bytes 14680064 | tf_op jit(solution)/shard_map/all_to_all | solution.py:116
  359.6 72.1 %while.18 = (s32[]{:T(128)}, f32[8,256]{1,0:T(8,128)S(1)}, f32[8,256]{1,0:T(8,128)S(1)}, f32[8,256,224]{1,2,0:T(8,128)}, s32[4]{0:T(128)S(1)}, /*index=5*/s32[25...) while((s32[]{:T(128)}, f32[8,256]{1,0:T(8,128)S(1)}, ...), condition=%wide.region_8.9_spmd.clone, body=%wide.region_4.8_spmd.clone.sunk | while | flops 955204608 | bytes 32524004 | solution.py:133
  359.6 0.1 convert_reduce_fusion.3
  359.7 0.3 and_or_fusion.2
  360.0 1.6 constant_dynamic-slice_fusion.4
  361.6 3.2 fusion.45
  364.8 3.2 fusion.46
  368.0 1.6 constant_dynamic-slice_fusion.5
  369.6 2.3 copy.78
  371.9 5.3 fusion.48
  377.2 0.1 convert_reduce_fusion.3
  377.3 0.3 and_or_fusion.2
  377.6 1.6 constant_dynamic-slice_fusion.4
  379.2 3.2 fusion.45
  382.4 3.2 fusion.46
  385.6 1.6 constant_dynamic-slice_fusion.5
  387.2 2.3 copy.78
  389.6 5.8 %fusion.48 = f32[8,256,224]{1,2,0:T(8,128)} fusion(f32[8,256,224]{1,2,0:T(8,128)} %get-tuple-element.367, bf16[512,8,224]{0,2,1:T(8,128)(2,1)} %bitcast.72, f32[8,512,256]{2,1,0:T(8,128)} %get-tuple-element.347, f32[8,256]{1,0:T(8,128)S(1)} %select_maximum_fusion.2, pred[256,512]{0,1:T(8,128)(4,1)S(1)} %and_or_fusion.2, ...), kind=kOutput, calls=%fused_computation.13.clone.1 | convolution fusion | flops 476381184 | bytes 9846785 | tf_op jit(solution)/shard_map/while/body/eval_jaxpr/eva,ael->evl/dot_general | solution.py:85
  395.4 0.1 convert_reduce_fusion.3
  395.5 0.3 and_or_fusion.2
  395.8 1.6 constant_dynamic-slice_fusion.4
  397.4 3.2 fusion.45
  400.6 3.2 fusion.46
  403.8 1.6 constant_dynamic-slice_fusion.5
  405.4 2.3 copy.78
  407.7 5.8 %fusion.48 = f32[8,256,224]{1,2,0:T(8,128)} fusion(f32[8,256,224]{1,2,0:T(8,128)} %get-tuple-element.367, bf16[512,8,224]{0,2,1:T(8,128)(2,1)} %bitcast.72, f32[8,512,256]{2,1,0:T(8,128)} %get-tuple-element.347, f32[8,256]{1,0:T(8,128)S(1)} %select_maximum_fusion.2, pred[256,512]{0,1:T(8,128)(4,1)S(1)} %and_or_fusion.2, ...), kind=kOutput, calls=%fused_computation.13.clone.1 | convolution fusion | flops 476381184 | bytes 9846785 | tf_op jit(solution)/shard_map/while/body/eval_jaxpr/eva,ael->evl/dot_general | solution.py:85
  413.5 0.1 convert_reduce_fusion.3
  413.6 0.3 and_or_fusion.2
  413.9 1.6 constant_dynamic-slice_fusion.4
  415.5 3.2 fusion.45
  418.7 3.2 fusion.46
  421.9 1.6 constant_dynamic-slice_fusion.5
  423.6 2.3 copy.78
  425.9 5.8 %fusion.48 = f32[8,256,224]{1,2,0:T(8,128)} fusion(f32[8,256,224]{1,2,0:T(8,128)} %get-tuple-element.367, bf16[512,8,224]{0,2,1:T(8,128)(2,1)} %bitcast.72, f32[8,512,256]{2,1,0:T(8,128)} %get-tuple-element.347, f32[8,256]{1,0:T(8,128)S(1)} %select_maximum_fusion.2, pred[256,512]{0,1:T(8,128)(4,1)S(1)} %and_or_fusion.2, ...), kind=kOutput, calls=%fused_computation.13.clone.1 | convolution fusion | flops 476381184 | bytes 9846785 | tf_op jit(solution)/shard_map/while/body/eval_jaxpr/eva,ael->evl/dot_general | solution.py:85
  431.7 1.6 divide_convert_fusion
  433.3 1.4 copy.72
  434.7 73.8 %all-to-all-done.2 = bf16[2,1,256,7168]{2,0,1,3:T(2,128)(2,1)} async-done(((bf16[2,1,256,7168]{2,0,1,3:T(2,128)(2,1)}), bf16[2,1,256,7168]{2,0,1,3:T(2,128)(2,1)}, u32[]{:S(2)}, u32[]{:S(2)}) %all-to-all-start.2) | async-done | bytes 7340064 | tf_op jit(solution)/shard_map/all_to_all | solution.py:143
  508.5 7.0 %copy.70 = bf16[2,1,256,7168]{2,3,0,1:T(8,128)(2,1)} copy(bf16[2,1,256,7168]{2,0,1,3:T(2,128)(2,1)} %all-to-all-done.2) | data formatting | bytes 14680064 | tf_op jit(solution)/shard_map/all_to_all | solution.py:143
  515.5 11.1 %copy.71 = bf16[2,1,8,256,896]{4,3,2,0,1:T(8,128)(2,1)} copy(bf16[2,1,8,256,896]{3,4,2,0,1:T(8,128)(2,1)} %bitcast.76) | data formatting | bytes 14680064 | tf_op jit(solution)/shard_map/all_to_all | solution.py:143
  526.6 5.6 %fusion.19 = (bf16[1,1,1024,896]{3,2,1,0:T(8,128)(2,1)}, bf16[1,1,1024,896]{3,2,1,0:T(8,128)(2,1)}) fusion(s32[]{:T(128)S(6)} %add.111, s32[]{:T(128)S(6)} %select_n.53, bf16[2,1,2048,896]{3,2,0,1:T(8,128)(2,1)} %bitcast.77), kind=kLoop, calls=%fused_computation.32 | loop fusion | bytes 11010056
  (52 shorter events, 0.4 us)
Async XLA Ops:
  7.2 5.4 %copy-start.1 = (bf16[1,256,1792]{2,1,0:T(8,128)(2,1)S(1)}, bf16[1,256,1792]{2,1,0:T(8,128)(2,1)}, u32[]{:S(2)}) copy-start(bf16[1,256,1792]{2,1,0:T(8,128)(2,1)} %param.10) | copy-start | bytes 2752516
  12.0 4.8 copy-start
  20.3 5.7 %copy-start.2 = (bf16[1,256,1792]{2,1,0:T(8,128)(2,1)S(1)}, bf16[1,256,1792]{2,1,0:T(8,128)(2,1)}, u32[]{:S(2)}) copy-start(bf16[1,256,1792]{2,1,0:T(8,128)(2,1)} %param.10) | copy-start | bytes 2752516
  20.3 89.1 %all-to-all-start.1 = ((bf16[2,4,256,1792]{2,3,0,1:T(8,128)(2,1)}), bf16[2,4,256,1792]{2,3,0,1:T(8,128)(2,1)}, u32[]{:S(2)}, u32[]{:S(2)}) async-start(bf16[2,4,256,1792]{2,3,0,1:T(8,128)(2,1)} %broadcast_select_fusion), calls=%async_computation.1 | async-start | bytes 14680064 | tf_op jit(solution)/shard_map/all_to_all | solution.py:144
  112.8 8.6 %copy-start.3 = (bf16[1,256,1792]{2,1,0:T(8,128)(2,1)S(1)}, bf16[1,256,1792]{2,1,0:T(8,128)(2,1)}, u32[]{:S(2)}) copy-start(bf16[1,256,1792]{2,1,0:T(8,128)(2,1)} %param.8) | copy-start | bytes 2752516
  112.8 9.1 %copy-start.5 = (s32[1,4]{1,0:T(1,128)S(1)}, s32[1,4]{1,0:T(1,128)}, u32[]{:S(2)}) copy-start(s32[1,4]{1,0:T(1,128)} %param.13) | copy-start | bytes 52
  112.8 9.7 %copy-start.4 = (s32[1,4]{1,0:T(1,128)S(1)}, s32[1,4]{1,0:T(1,128)}, u32[]{:S(2)}) copy-start(s32[1,4]{1,0:T(1,128)} %param.11) | copy-start | bytes 52
  112.8 215.6 %all-to-all-start = ((bf16[8,256,1792]{1,2,0:T(8,128)(2,1)}), bf16[8,256,1792]{1,2,0:T(8,128)(2,1)}, u32[]{:S(2)}, u32[]{:S(2)}) async-start(bf16[8,256,1792]{1,2,0:T(8,128)(2,1)} %stack.6), calls=%async_computation | async-start | bytes 14680064 | tf_op jit(solution)/shard_map/all_to_all | solution.py:116
  120.6 239.0 %all-gather.2.cloned.1.call-start = ((), (), s32[]{:S(2)}) async-start(), calls=%async_computation.3 | async-start | bytes 8257536 | tf_op jit(solution)/shard_map/all_gather | solution.py:114
  328.4 180.1 %all-to-all-start.2 = ((bf16[2,1,256,7168]{2,0,1,3:T(2,128)(2,1)}), bf16[2,1,256,7168]{2,0,1,3:T(2,128)(2,1)}, u32[]{:S(2)}, u32[]{:S(2)}) async-start(bf16[2,1,256,7168]{2,0,1,3:T(2,128)(2,1)} %copy.69), calls=%async_computation.2 | async-start | bytes 14680064 | tf_op jit(solution)/shard_map/all_to_all | solution.py:143
Sparse Core Ops, SparseCore 0:
  123.7 229.8 all-gather.1
